TPU v7x, 32 devices: a whole 2x2x4 slice. The times are simulated.
32 devices in a mesh: grp: 2 (over y), col: 4 (over z), row: 2 (over x), limb: 2 (over core).
Axes of the slice: x: 2, y: 2, z: 4, core: 2. Of those that a mesh axis runs over, the one named last changes fastest.
Arguments:
- database: bfloat16 [8192, 8192], P(('grp', 'row'), 'col'), parts along dimension 0, may hold values from -128 to 127, as said below
- lwe_matrix: bfloat16 [8192, 2, 512], P('col', 'limb'), may hold values from -0.0008544922 to 0.0008544922
- secret_ct: float32 [2, 2, 2, 512, 4096], P(None, None, 'limb', 'col', 'row'), may hold values from -6 to 6
Outputs:
- encrypted_product: float32 [4, 2, 4096], P('grp', None, 'row'), parts along dimension 0
There are 2 independent parts, one for each index of `grp`. A program takes and returns all parts, laid end to end along the dimension named above; an argument that names none is the same for every part. Nothing has to cross between parts.
Inputs may be any that keep to these rules, and one draw needn't show every extreme that they name: `database`: whole numbers.
All inputs are finite; a program needn't handle non-finite values.
Results may differ from a plain program's by a relative error of at most 0.0003.
Values sent between devices are 32-bit elements; how exact they have to be, the bound alone decides.
A program may use at most 64 MiB of HBM per device.

v0:
```python
import math

import jax
import jax.numpy as jnp
from jax import lax
from jax.sharding import PartitionSpec as P


def exact_dot(left, right):
    return jnp.dot(left, right, precision=lax.Precision.HIGHEST, preferred_element_type=jnp.float32)


def body(database, lwe_matrix, secret_ct):
    row_count = lax.axis_size("row")
    row_rank = lax.axis_index("row")
    row_dev = database.shape[0]
    degree_all = row_dev * row_count
    sub_rows = row_dev // row_count
    a_panel = lwe_matrix[:, 0, :]
    contract_rows = (((0,), (1,)), ((), ()))
    hint_block = lax.psum_scatter(
        lax.dot_general(a_panel, database, contract_rows, preferred_element_type=jnp.float32),
        "col",
        scatter_dimension=0,
        tiled=True,
    )
    freq_low = jnp.arange(row_count, dtype=jnp.int32)
    odd_index = 2 * freq_low + 1
    by_columns = lax.all_to_all(
        hint_block[:, None, :], "row", split_axis=2, concat_axis=1, tiled=True
    )
    phase_index = freq_low[:, None] * odd_index[None, :] % (2 * row_count)
    angle_small = jnp.pi * phase_index.astype(jnp.float32) / row_count
    mixed_real = jnp.einsum(
        "jas,ak->jks", by_columns, jnp.cos(angle_small), precision=lax.Precision.HIGHEST
    )
    mixed_imag = -jnp.einsum(
        "jas,ak->jks", by_columns, jnp.sin(angle_small), precision=lax.Precision.HIGHEST
    )
    local_rows = row_rank * sub_rows + jnp.arange(sub_rows, dtype=jnp.int32)
    twist_index = odd_index[:, None] * local_rows[None, :] % (2 * degree_all)
    twist_angle = jnp.pi * twist_index.astype(jnp.float32) / degree_all
    twist_cos = jnp.cos(twist_angle)
    twist_sin = jnp.sin(twist_angle)
    turned_real = mixed_real * twist_cos + mixed_imag * twist_sin
    turned_imag = mixed_imag * twist_cos - mixed_real * twist_sin
    back_rows = lax.all_to_all(
        jnp.stack([turned_real, turned_imag]), "row", split_axis=2, concat_axis=3, tiled=True
    )
    point_real = back_rows[0, :, 0, :]
    point_imag = back_rows[1, :, 0, :]
    freq_rows = jnp.arange(row_dev, dtype=jnp.int32)
    table_index = freq_rows[:, None] * freq_rows[None, :] % row_dev
    table_angle = 2.0 * jnp.pi * table_index.astype(jnp.float32) / row_dev
    table_cos = jnp.cos(table_angle)
    table_sin = jnp.sin(table_angle)
    scale_factor = 1.0 / math.sqrt(degree_all)
    spec_real = (exact_dot(point_real, table_cos) + exact_dot(point_imag, table_sin)) * scale_factor
    spec_imag = (exact_dot(point_imag, table_cos) - exact_dot(point_real, table_sin)) * scale_factor
    cipher = secret_ct[:, :, 0]
    prod_real = jnp.sum(spec_real * cipher[:, 0] - spec_imag * cipher[:, 1], axis=1)
    prod_imag = jnp.sum(spec_real * cipher[:, 1] + spec_imag * cipher[:, 0], axis=1)
    slot_total = lax.psum(jnp.stack([prod_real, prod_imag], axis=1), ("col", "limb"))
    return slot_total / math.sqrt(2 * lwe_matrix.shape[2])


def solution(mesh):
    placed = (P(("grp", "row"), "col"), P("col", "limb", None), P(None, None, "limb", "col", "row"))
    return jax.shard_map(
        body, mesh=mesh, in_specs=placed, out_specs=P("grp", None, "row"), check_vma=False
    )
```

profile of v0, /device:TPU:0, one launch (start us, length us, event | category | flops | bytes accessed | tf_op | source)
XLA Modules:
  0.0 507.2 jit_solution(10724719638266237290)
XLA Ops:
  6.5 0.0 copy-start
  6.5 0.0 reduce-scatter.2.cloned.1.call-start
  6.5 1.6 copy-done
  8.1 9.6 %fusion.28 = f32[512,2048]{1,0:T(8,128)} fusion(bf16[2048,2048]{1,0:T(8,128)(2,1)} %param.3, bf16[2048,1,512]{2,0,1:T(8,128)(2,1)S(1)} %copy-done), kind=kOutput, calls=%fused_computation.22 | convolution fusion | flops 4294967296 | bytes 14680064 | tf_op jit(solution)/shard_map/dot_general | solution.py:22
  17.7 0.0 reduce-scatter.2.cloned.1.call-update
  17.8 79.7 %reduce-scatter.2.cloned.1.call-done = f32[128,2048]{1,0:T(8,128)} async-done(((f32[512,2048]{1,0:T(8,128)}), f32[128,2048]{1,0:T(8,128)}) %reduce-scatter.2.cloned.1.call-update) | async-done | bytes 1048592 | tf_op jit(solution)/shard_map/reduce_scatter | solution.py:21
  97.4 3.6 copy.12
  101.0 3.6 all-to-all-start
  104.6 0.2 fusion.34
  104.8 13.3 %all-to-all-done = f32[128,1,2048]{0,1,2:T(1,128)S(1)} async-done(((f32[128,1,2048]{0,1,2:T(1,128)}), f32[128,1,2048]{0,1,2:T(1,128)S(1)}, u32[]{:S(2)}, u32[]{:S(2)}) %all-to-all-start) | async-done | bytes 1048608 | tf_op jit(solution)/shard_map/all_to_all | solution.py:29
  118.1 0.0 copy-start.2
  118.1 1.0 copy-done.2
  119.1 1.6 copy.19
  120.7 3.9 convolution_negate_fusion
  124.6 4.7 add_bitcast_fusion
  129.4 0.9 pad_maximum_fusion
  130.3 0.7 copy.14
  131.0 27.0 %all_to_all.21 = f32[2,128,2,1024]{3,1,0,2:T(8,128)S(1)} all-to-all(f32[2,128,2,1024]{3,1,0,2:T(8,128)S(1)} %copy.14), channel_id=1, replica_groups=mesh['grp'=2,'col'=4,'row'=2,'limb'=2] {'row'}, dimensions={2} | all-to-all | bytes 4194304 | tf_op jit(solution)/shard_map/all_to_all | solution.py:47
  157.9 1.2 fusion.69
  159.1 2.5 copy.21
  161.7 77.7 %fusion.8 = f32[128,2048]{1,0:T(8,128)} fusion(f32[128,2048]{0,1:T(8,128)} %bitcast.52), kind=kOutput, calls=%fused_computation.11 | convolution fusion | flops 6501171200 | bytes 2097152 | tf_op jit(solution)/shard_map/dot_general | solution.py:10
  239.4 1.3 copy.20
  240.7 0.0 copy-start.4
  240.7 0.0 copy-start.5
  240.7 77.3 %fusion.10 = f32[128,2048]{1,0:T(8,128)S(1)} fusion(f32[128,2048]{0,1:T(8,128)} %bitcast.55), kind=kOutput, calls=%fused_computation.12 | convolution fusion | flops 6501171200 | bytes 2097152 | tf_op jit(solution)/shard_map/dot_general | solution.py:10
  318.1 0.0 copy-done.4
  318.1 0.0 copy-done.5
  318.1 0.0 copy-start.3
  318.1 76.5 %fusion.22 = f32[128,2048]{1,0:T(8,128)S(1)} fusion(f32[128,2048]{1,0:T(8,128)S(1)} %copy-done.5, f32[128,2048]{0,1:T(8,128)S(1)} %bitcast.56), kind=kOutput, calls=%fused_computation.17 | convolution fusion | flops 6501695488 | bytes 3145728 | tf_op jit(solution)/shard_map/dot_general | solution.py:10
  394.6 0.0 copy-done.3
  394.7 0.0 copy-start.1
  394.7 76.6 %fusion.25 = f32[128,2048]{1,0:T(8,128)S(1)} fusion(f32[128,2048]{1,0:T(8,128)S(1)} %fusion.10, f32[128,2048]{0,1:T(8,128)S(1)} %bitcast.53), kind=kOutput, calls=%fused_computation.18 | convolution fusion | flops 6501695488 | bytes 3145728 | tf_op jit(solution)/shard_map/dot_general | solution.py:10
  471.3 0.0 copy-done.1
  471.3 0.8 subtract_reduce_fusion
  472.1 27.1 %psum.7 = f32[2,2,2048]{2,0,1:T(2,128)S(1)} all-reduce(f32[2,2,2048]{2,0,1:T(2,128)S(1)} %pad_maximum_fusion.1), channel_id=1, replica_groups=mesh['grp'=2,'col'=4,'row'=2,'limb'=2] {'col','limb'}, use_global_device_ids=true, to_apply=%region_3.4 | all-reduce | flops 8192 | bytes 65536 | tf_op jit(solution)/shard_map/psum | solution.py:63
  499.3 0.6 copy.18
  (4 shorter events, 0.0 us)
Async XLA Ops:
  6.5 1.6 copy-start
  6.5 90.9 %reduce-scatter.2.cloned.1.call-start = ((), (), s32[]{:S(2)}) async-start(), calls=%async_computation.3 | async-start | bytes 5242880 | tf_op jit(solution)/shard_map/reduce_scatter | solution.py:21
  101.0 17.1 %all-to-all-start = ((f32[128,1,2048]{0,1,2:T(1,128)}), f32[128,1,2048]{0,1,2:T(1,128)S(1)}, u32[]{:S(2)}, u32[]{:S(2)}) async-start(f32[128,1,2048]{0,1,2:T(1,128)} %copy.12), calls=%async_computation.1 | async-start | bytes 2097152 | tf_op jit(solution)/shard_map/all_to_all | solution.py:29
  118.1 1.0 copy-start.2
  240.7 77.3 %copy-start.4 = (f32[1,128,2,1024]{1,3,2,0:T(8,128)S(1)}, f32[1,128,2,1024]{1,3,2,0:T(8,128)}, u32[]{:S(2)}) copy-start(f32[1,128,2,1024]{1,3,2,0:T(8,128)} %copy.20) | copy-start | bytes 3145732
  240.7 77.4 %copy-start.5 = (f32[128,2048]{1,0:T(8,128)S(1)}, f32[128,2048]{1,0:T(8,128)}, u32[]{:S(2)}) copy-start(f32[128,2048]{1,0:T(8,128)} %fusion.8) | copy-start | bytes 3145732
  318.1 76.6 %copy-start.3 = (f32[1,128,2,1024]{1,3,2,0:T(8,128)S(1)}, f32[1,128,2,1024]{1,3,2,0:T(8,128)}, u32[]{:S(2)}) copy-start(f32[1,128,2,1024]{1,3,2,0:T(8,128)} %copy.21) | copy-start | bytes 3145732
  394.7 76.6 %copy-start.1 = (f32[2,2,1,128,2048]{4,3,2,1,0:T(8,128)S(1)}, f32[2,2,1,128,2048]{4,3,2,1,0:T(8,128)}, u32[]{:S(2)}) copy-start(f32[2,2,1,128,2048]{4,3,2,1,0:T(8,128)} %param.5) | copy-start | bytes 12582916
Sparse Core Ops, SparseCore 0:
  17.9 79.5 reduce-scatter.1
where the time goes:
time: 514 us; the launch traced here: 507 us
  matrix products  326 us (63%)
  waiting for transfers between devices  93 us (18%)
  blocking collectives  54.1 us (11%)
  local copies, waits for them, and re-layouts  14.1 us (3%)
  between operations  14 us (3%)
    dot_general x4, matrix products, exact_dot(): jnp.dot(left, right, precision=lax.Precision.HIGHEST, preferred_element_t...  308 us
    reduce_scatter x1, waiting for transfers between devices, body(): lax.psum_scatter(lax.dot_general(a_panel, database, contract_rows, prefer...  79.7 us
    psum x1, blocking collectives, body(): lax.psum(jnp.stack([prod_real, prod_imag], axis=1), ('col', 'limb'))  27.1 us
    all_to_all x1, blocking collectives, body(): lax.all_to_all(jnp.stack([turned_real, turned_imag]), 'row', split_axis=2...  27 us
    all_to_all x1, waiting for transfers between devices, body(): lax.all_to_all(hint_block[:, None, :], 'row', split_axis=2, concat_axis=1...  13.3 us
  transfers between devices with their start and end apart: 2, of which 2 were waited for; matrix products, arithmetic and copies ran while one was open for 0% of the time, Pallas kernels for 0%

commit v1 on v0

v1 whole, which is shorter than its diff:
```python
import math

import jax
import jax.numpy as jnp
import numpy as np
from jax import lax
from jax.sharding import PartitionSpec as P

CHUNKS = 4


def tables(row_count, row_dev, fast):
    slow = row_dev // fast
    degree = row_count * row_dev
    m = np.arange(row_dev)
    t = np.arange(fast)
    angle = -2.0 * np.pi * (m[:, None] * t[None, :] % row_dev) / row_dev
    first = np.exp(1j * angle).reshape(fast, slow, fast).transpose(1, 0, 2)
    a = np.arange(row_count)
    n = np.arange(degree)
    turn = -np.pi * (n[None, :] * (2 * a[:, None] + 1) % (2 * degree)) / degree
    turn = np.exp(1j * turn).reshape(row_count, row_count, fast, slow).transpose(0, 3, 1, 2)
    v = np.arange(slow)
    last = np.exp(-2j * np.pi * (v[:, None] * v[None, :] % slow) / slow)
    last = np.stack([np.stack([last.real, last.imag], 0), np.stack([-last.imag, last.real], 0)], 0)
    return first, turn, last.astype(np.float32)


def body(database, lwe_matrix, secret_ct):
    row_count = lax.axis_size("row")
    row_rank = lax.axis_index("row")
    col_count = lax.axis_size("col")
    row_dev = database.shape[0]
    half = lwe_matrix.shape[2]
    own = half // col_count
    part = own // CHUNKS
    fast = 128
    slow = row_dev // fast
    first, turn, last = tables(row_count, row_dev, fast)
    f_re = jnp.asarray(first.real, jnp.float32)[:, None]
    f_im = jnp.asarray(first.imag, jnp.float32)[:, None]
    g_re = lax.dynamic_index_in_dim(jnp.asarray(turn.real, jnp.float32), row_rank, 0, False)[..., None]
    g_im = lax.dynamic_index_in_dim(jnp.asarray(turn.imag, jnp.float32), row_rank, 0, False)[..., None]
    stage = jnp.stack([f_re * g_re - f_im * g_im, f_re * g_im + f_im * g_re], axis=3)
    stage = stage.reshape(slow, row_count, fast, 2, fast)
    panel = lwe_matrix[:, 0, :].reshape(-1, col_count, own)
    scale = 1.0 / (math.sqrt(row_dev * row_count) * math.sqrt(2 * half))
    prod_real = prod_imag = 0.0
    for k in range(CHUNKS):
        piece = panel[:, :, k * part : (k + 1) * part].reshape(-1, col_count * part)
        partial = lax.dot_general(
            piece, database, (((0,), (1,)), ((), ())), preferred_element_type=jnp.float32
        )
        mine = lax.psum_scatter(partial, "col", scatter_dimension=0, tiled=True)
        blocks = [mine]
        for step in range(1, row_count):
            perm = [(i, (i + step) % row_count) for i in range(row_count)]
            blocks.append(lax.ppermute(mine, "row", perm))
        total = 0.0
        for step, block in enumerate(blocks):
            source = (row_rank - step) % row_count
            table = lax.dynamic_index_in_dim(stage, source, 1, False)
            total = total + jnp.einsum(
                "juv,vuct->vjct",
                block.reshape(part, fast, slow),
                table,
                precision=lax.Precision.HIGH,
                preferred_element_type=jnp.float32,
            )
        spec = jnp.einsum("vjct,cdvs->djst", total, last, precision=lax.Precision.HIGH)
        spec = spec.reshape(2, part, row_dev)
        cipher = secret_ct[:, :, 0, k * part : (k + 1) * part]
        prod_real += jnp.sum(spec[0] * cipher[:, 0] - spec[1] * cipher[:, 1], axis=1)
        prod_imag += jnp.sum(spec[0] * cipher[:, 1] + spec[1] * cipher[:, 0], axis=1)
    return lax.psum(jnp.stack([prod_real, prod_imag], axis=1) * scale, ("col", "limb"))


def solution(mesh):
    placed = (P(("grp", "row"), "col"), P("col", "limb", None), P(None, None, "limb", "col", "row"))
    return jax.shard_map(
        body, mesh=mesh, in_specs=placed, out_specs=P("grp", None, "row"), check_vma=False
    )
```

time: 514 us -> 195 us (0.38); the launches traced: 507 us -> 194 us
  matrix products: 326 us -> 50.9 us
  waiting for transfers between devices: 93 us -> 52.5 us
  blocking collectives: 54.1 us -> 25.9 us
  other arithmetic: 1.98 us -> 18.3 us
  local copies, waits for them, and re-layouts: 14.1 us -> 25.3 us
    dot_general x7 -> x16, matrix products: 326 us -> 50.9 us  [the longest x4 29.6 us: body(): lax.dot_general(piece, database, (((0,), (1,)), ((), ())), preferred_elem...]
    reduce_scatter x1 -> x4, waiting for transfers between devices: 79.7 us -> 52.4 us  [body(): mine = lax.psum_scatter(partial, 'col', scatter_dimension=0, tiled=True)]
    all_to_all x1 -> x0, blocking collectives: 27 us -> none  [body(): lax.all_to_all(jnp.stack([turned_real, turned_imag]), 'row', split_axis=2...]
    all_to_all x1 -> x0, waiting for transfers between devices: 13.3 us -> none  [body(): lax.all_to_all(hint_block[:, None, :], 'row', split_axis=2, concat_axis=1...]
    add x2 -> x3, other arithmetic: 0.01 us -> 10.8 us  [the longest x1 10.7 us: body(): f_re * g_im + f_im * g_re]
    reduce_scatter x0 -> x4, local copies, waits for them, and re-layouts: none -> 7.35 us  [body(): mine = lax.psum_scatter(partial, 'col', scatter_dimension=0, tiled=True)]
    ppermute x0 -> x4, starting transfers between devices: none -> 7.24 us  [body(): blocks.append(lax.ppermute(mine, 'row', perm))]
    squeeze x0 -> x1, other arithmetic: none -> 6.51 us  [body(): table = lax.dynamic_index_in_dim(stage, source, 1, False)]
  transfers between devices with their start and end apart: 2 -> 8, of which waited for: 2 -> 3; matrix products, arithmetic and copies ran while one was open for 0% -> 39% of each run, Pallas kernels for 0% -> 0%
where the time goes in v1:
time: 195 us; the launch traced here: 194 us
  waiting for transfers between devices  52.5 us (27%)
  matrix products  50.9 us (26%)
  blocking collectives  25.9 us (13%)
  local copies, waits for them, and re-layouts  25.3 us (13%)
  other arithmetic  18.3 us (9%)
  between operations  13.6 us (7%)
  starting transfers between devices  7.37 us (4%)
    reduce_scatter x4, waiting for transfers between devices, body(): mine = lax.psum_scatter(partial, 'col', scatter_dimension=0, tiled=True)  52.4 us
    dot_general x4, matrix products, body(): lax.dot_general(piece, database, (((0,), (1,)), ((), ())), preferred_elem...  29.6 us
    psum x1, blocking collectives, body(): lax.psum(jnp.stack([prod_real, prod_imag], axis=1) * scale, ('col', 'limb'))  25.9 us
    dot_general x8, matrix products, body(): jnp.einsum('juv,vuct->vjct', block.reshape(part, fast, slow), table, prec...  17.5 us
    add x1, other arithmetic, body(): f_re * g_im + f_im * g_re  10.7 us
    unnamed x63, local copies, waits for them, and re-layouts  8.37 us
    reduce_scatter x4, local copies, waits for them, and re-layouts, body(): mine = lax.psum_scatter(partial, 'col', scatter_dimension=0, tiled=True)  7.35 us
    ppermute x4, starting transfers between devices, body(): blocks.append(lax.ppermute(mine, 'row', perm))  7.24 us
  transfers between devices with their start and end apart: 8, of which 3 were waited for; matrix products, arithmetic and copies ran while one was open for 39% of the time, Pallas kernels for 0%

profile of v1, /device:TPU:0, one launch (start us, length us, event | category | flops | bytes accessed | tf_op | source)
XLA Modules:
  0.0 194.0 jit_solution(14981095304729488325)
XLA Ops:
  6.5 2.9 %copy.16 = bf16[2048,1,512]{0,2,1:T(8,128)(2,1)S(1)} copy(bf16[2048,1,512]{2,0,1:T(8,128)(2,1)} %param.12) | data formatting | bytes 4194304 | tf_op args[1]
  9.5 1.0 fusion.36
  10.5 7.4 %fusion.41 = f32[128,2048]{1,0:T(8,128)} fusion(bf16[2048,128]{0,1:T(8,128)(2,1)S(1)} %bitcast.218, bf16[2048,2048]{1,0:T(8,128)(2,1)} %param.11), kind=kOutput, calls=%fused_computation.88 | convolution fusion | flops 1073741824 | bytes 9961472 | tf_op jit(solution)/shard_map/dot_general | solution.py:51
  18.0 7.2 %fusion.42 = f32[128,2048]{1,0:T(8,128)} fusion(bf16[2048,128]{0,1:T(8,128)(2,1)S(1)} %bitcast.217, bf16[2048,2048]{1,0:T(8,128)(2,1)} %param.11), kind=kOutput, calls=%fused_computation.89 | convolution fusion | flops 1073741824 | bytes 9961472 | tf_op jit(solution)/shard_map/dot_general | solution.py:51
  25.3 7.5 %fusion.43 = f32[128,2048]{1,0:T(8,128)} fusion(bf16[2048,128]{0,1:T(8,128)(2,1)S(1)} %bitcast.216, bf16[2048,2048]{1,0:T(8,128)(2,1)} %param.11), kind=kOutput, calls=%fused_computation.90 | convolution fusion | flops 1073741824 | bytes 9961472 | tf_op jit(solution)/shard_map/dot_general | solution.py:51
  32.9 7.5 %fusion.44 = f32[128,2048]{1,0:T(8,128)} fusion(bf16[2048,128]{0,1:T(8,128)(2,1)S(1)} %bitcast.215, bf16[2048,2048]{1,0:T(8,128)(2,1)} %param.11), kind=kOutput, calls=%fused_computation.91 | convolution fusion | flops 1073741824 | bytes 9961472 | tf_op jit(solution)/shard_map/dot_general | solution.py:51
  40.4 10.7 %multiply_add_fusion = (f32[16,2,128,1,128]{4,3,2,1,0:T(1,128)}, f32[16,2,128,1,128]{4,3,2,1,0:T(1,128)}) fusion(f32[16,2,128]{2,1,0:T(2,128)S(1)} %dynamic-slice_bitcast_fusion, f32[16,128,128]{2,1,0:T(8,128)S(1)} %copy-done.23, f32[16,2,128]{2,1,0:T(2,128)S(1)} %dynamic-slice_bitcast_fusion.1, f32[16,128,128]{2,1,0:T(8,128)S(1)} %copy-done.22), kind=kLoop, calls=%fused_computation.8 | loop fusion | flops 3145728 | bytes 6324224 | tf_op jit(solution)/shard_map/add | solution.py:44
  51.2 6.5 %fusion.3 = (f32[16,128,2,128]{3,2,1,0:T(2,128)}, f32[16,128,2,128]{3,2,1,0:T(2,128)S(1)}) fusion(s32[]{:T(128)S(6)} %select_n.43, f32[16,2,128,1,128]{4,3,2,1,0:T(1,128)} %get-tuple-element.20, f32[16,2,128,1,128]{4,3,2,1,0:T(1,128)} %get-tuple-element.19, s32[]{:T(128)S(6)} %select_n.45), kind=kLoop, calls=%fused_computation.7 | loop fusion | flops 1048576 | bytes 8388616 | tf_op jit(solution)/shard_map/jit(dynamic_index_in_dim)/squeeze | solution.py:62
  57.7 2.1 %slice_bitcast_fusion.2 = (f32[2,2,32,2048]{3,2,1,0:T(8,128)}, f32[2,2,32,2048]{3,2,1,0:T(8,128)}, f32[2,2,32,2048]{3,2,1,0:T(8,128)}, f32[2,2,32,2048]{3,2,1,0:T(8,128)}) fusion(f32[2,2,1,128,2048]{4,3,2,1,0:T(8,128)S(1)} %copy-done.3), kind=kLoop, calls=%fused_computation.40 | loop fusion | bytes 8388608 | tf_op jit(solution)/shard_map/squeeze | solution.py:72
  59.7 2.8 %collective-permute-start = (f32[32,2048]{1,0:T(8,128)}, f32[32,2048]{1,0:T(8,128)}, u32[]{:S(2)}, u32[]{:S(2)}) collective-permute-start(f32[32,2048]{1,0:T(8,128)} %reduce-scatter.5.cloned.1.call-done), channel_id=1, source_target_pairs={{0,2},{2,0},{1,3},{3,1},{4,6},{6,4},{5,7},{7,5},{8,10},{10,8},{9,1... | collective-permute-start | bytes 786440 | tf_op jit(solution)/shard_map/ppermute | solution.py:58
  62.5 1.3 copy.17
  63.9 12.3 %reduce-scatter.7.cloned.1.call-done = f32[32,2048]{1,0:T(8,128)} async-done(((f32[128,2048]{1,0:T(8,128)}), f32[32,2048]{1,0:T(8,128)}) %reduce-scatter.7.cloned.1.call-update) | async-done | bytes 262160 | tf_op jit(solution)/shard_map/reduce_scatter | solution.py:54
  76.2 1.5 collective-permute-start.1
  77.7 2.4 %copy.20 = f32[32,2048]{0,1:T(8,128)} copy(f32[32,2048]{1,0:T(8,128)} %reduce-scatter.7.cloned.1.call-done) | data formatting | bytes 524288 | tf_op jit(solution)/shard_map/reduce_scatter | solution.py:54
  80.1 24.2 %reduce-scatter.9.cloned.1.call-done = f32[32,2048]{1,0:T(8,128)} async-done(((f32[128,2048]{1,0:T(8,128)}), f32[32,2048]{1,0:T(8,128)}) %reduce-scatter.9.cloned.1.call-update) | async-done | bytes 262160 | tf_op jit(solution)/shard_map/reduce_scatter | solution.py:54
  104.3 1.5 collective-permute-start.2
  105.8 2.3 %copy.23 = f32[32,2048]{0,1:T(8,128)} copy(f32[32,2048]{1,0:T(8,128)} %reduce-scatter.9.cloned.1.call-done) | data formatting | bytes 524288 | tf_op jit(solution)/shard_map/reduce_scatter | solution.py:54
  108.1 3.8 %fusion.18 = f32[16,32,2,128]{3,1,2,0:T(8,128)} fusion(f32[16,128,2,128]{3,2,1,0:T(2,128)} %get-tuple-element.17, f32[32,128,16,1]{0,2,1,3:T(8,128)S(1)} %bitcast.207), kind=kOutput, calls=%fused_computation.24 | convolution fusion | flops 100663296 | bytes 2883584 | tf_op jit(solution)/shard_map/juv,vuct->vjct/dot_general | solution.py:63
  112.0 2.2 %fusion.16 = f32[16,32,2,128]{3,1,2,0:T(8,128)} fusion(f32[16,128,2,128]{3,2,1,0:T(2,128)S(1)} %copy-done, f32[32,128,16,1]{0,2,1,3:T(8,128)S(1)} %bitcast.208), kind=kOutput, calls=%fused_computation.22 | convolution fusion | flops 100663296 | bytes 2883584 | tf_op jit(solution)/shard_map/juv,vuct->vjct/dot_general | solution.py:63
  114.2 2.2 %fusion.14 = f32[16,32,2,128]{3,1,2,0:T(8,128)} fusion(f32[16,128,2,128]{3,2,1,0:T(2,128)S(1)} %copy-done, f32[32,128,16,1]{0,2,1,3:T(8,128)S(1)} %bitcast.209), kind=kOutput, calls=%fused_computation.20 | convolution fusion | flops 100663296 | bytes 2883584 | tf_op jit(solution)/shard_map/juv,vuct->vjct/dot_general | solution.py:63
  116.4 15.8 %reduce-scatter.11.cloned.1.call-done = f32[32,2048]{1,0:T(8,128)} async-done(((f32[128,2048]{1,0:T(8,128)}), f32[32,2048]{1,0:T(8,128)}) %reduce-scatter.11.cloned.1.call-update) | async-done | bytes 262160 | tf_op jit(solution)/shard_map/reduce_scatter | solution.py:54
  132.3 1.5 collective-permute-start.3
  133.8 1.3 copy.26
  135.1 3.7 %fusion.12 = f32[16,32,2,128]{3,1,2,0:T(8,128)} fusion(f32[16,128,2,128]{3,2,1,0:T(2,128)} %get-tuple-element.17, f32[32,128,16,1]{0,2,1,3:T(8,128)S(1)} %bitcast.212), kind=kOutput, calls=%fused_computation.18 | convolution fusion | flops 100663296 | bytes 2883584 | tf_op jit(solution)/shard_map/juv,vuct->vjct/dot_general | solution.py:63
  138.8 1.3 copy.18
  140.1 1.3 fusion.10
  141.4 1.0 convolution_bitcast_fusion.3
  142.4 0.8 fusion.38
  143.2 1.3 copy.21
  144.5 1.3 fusion.8
  145.9 1.0 convolution_bitcast_fusion.2
  146.9 0.8 fusion.37
  147.7 0.3 copy.24
  148.0 1.5 fusion.6
  149.6 1.0 convolution_bitcast_fusion.1
  150.7 0.8 copy.147
  151.5 0.8 copy.144
  152.3 0.8 copy.145
  153.2 0.8 copy.142
  153.9 0.8 copy.143
  154.7 1.3 copy.27
  156.0 1.3 fusion.4
  157.4 1.0 convolution_bitcast_fusion
  159.1 0.5 subtract_reduce_fusion.2
  159.8 0.3 copy-done.5
  160.3 0.5 subtract_reduce_fusion
  160.8 25.9 %psum.7 = f32[2,2,2048]{2,0,1:T(2,128)S(1)} all-reduce(f32[2,2,2048]{2,0,1:T(2,128)S(1)} %maximum_multiply_fusion), channel_id=1, replica_groups=mesh['grp'=2,'col'=4,'row'=2,'limb'=2] {'col','limb'}, use_global_device_ids=true, to_apply=%region_12.13 | all-reduce | flops 8192 | bytes 65536 | tf_op jit(solution)/shard_map/psum | solution.py:75
  186.8 0.6 copy.29
  (76 shorter events, 1.5 us)
Async XLA Ops:
  6.5 53.2 %reduce-scatter.5.cloned.1.call-start = ((), (), s32[]{:S(2)}) async-start(), calls=%async_computation.4 | async-start | bytes 1310720 | tf_op jit(solution)/shard_map/reduce_scatter | solution.py:54
  10.5 7.5 %copy-start.12 = (bf16[2048,4,32]{0,2,1:T(8,128)(2,1)S(1)}, bf16[2048,4,32]{0,2,1:T(8,128)(2,1)}, u32[]{:S(2)}) copy-start(bf16[2048,4,32]{0,2,1:T(8,128)(2,1)} %get-tuple-element.21) | copy-start | bytes 1572868
  17.9 58.3 %reduce-scatter.7.cloned.1.call-start = ((), (), s32[]{:S(2)}) async-start(), calls=%async_computation.5 | async-start | bytes 1310720 | tf_op jit(solution)/shard_map/reduce_scatter | solution.py:54
  25.2 79.1 %reduce-scatter.9.cloned.1.call-start = ((), (), s32[]{:S(2)}) async-start(), calls=%async_computation.6 | async-start | bytes 1310720 | tf_op jit(solution)/shard_map/reduce_scatter | solution.py:54
  32.8 99.5 %reduce-scatter.11.cloned.1.call-start = ((), (), s32[]{:S(2)}) async-start(), calls=%async_computation.7 | async-start | bytes 1310720 | tf_op jit(solution)/shard_map/reduce_scatter | solution.py:54
  32.8 7.5 %copy-start.26 = (f32[2,16,2,128]{3,2,1,0:T(2,128)S(1)}, f32[2,16,2,128]{3,2,1,0:T(2,128)}, u32[]{:S(2)}) copy-start(f32[2,16,2,128]{3,2,1,0:T(2,128)} %constant.77.clone) | copy-start | bytes 98308
  32.8 7.6 %copy-start.25 = (f32[2,16,2,128]{3,2,1,0:T(2,128)S(1)}, f32[2,16,2,128]{3,2,1,0:T(2,128)}, u32[]{:S(2)}) copy-start(f32[2,16,2,128]{3,2,1,0:T(2,128)} %constant.76.clone) | copy-start | bytes 98308
  32.8 7.6 %copy-start.22 = (f32[16,128,128]{2,1,0:T(8,128)S(1)}, f32[16,128,128]{2,1,0:T(8,128)}, u32[]{:S(2)}) copy-start(f32[16,128,128]{2,1,0:T(8,128)} %constant.74.clone) | copy-start | bytes 3145732
  32.9 7.6 %copy-start.23 = (f32[16,128,128]{2,1,0:T(8,128)S(1)}, f32[16,128,128]{2,1,0:T(8,128)}, u32[]{:S(2)}) copy-start(f32[16,128,128]{2,1,0:T(8,128)} %constant.75.clone) | copy-start | bytes 3145732
  51.2 6.5 %copy-start.3 = (f32[2,2,1,128,2048]{4,3,2,1,0:T(8,128)S(1)}, f32[2,2,1,128,2048]{4,3,2,1,0:T(8,128)}, u32[]{:S(2)}) copy-start(f32[2,2,1,128,2048]{4,3,2,1,0:T(8,128)} %param.13) | copy-start | bytes 12582916
  59.7 79.0 %collective-permute-start = (f32[32,2048]{1,0:T(8,128)}, f32[32,2048]{1,0:T(8,128)}, u32[]{:S(2)}, u32[]{:S(2)}) collective-permute-start(f32[32,2048]{1,0:T(8,128)} %reduce-scatter.5.cloned.1.call-done), channel_id=1, source_target_pairs={{0,2},{2,0},{1,3},{3,1},{4,6},{6,4},{5,7},{7,5},{8,10},{10,8},{9,1... | collective-permute-start | bytes 786440 | tf_op jit(solution)/shard_map/ppermute | solution.py:58
  76.2 67.1 %collective-permute-start.1 = (f32[32,2048]{1,0:T(8,128)}, f32[32,2048]{1,0:T(8,128)}, u32[]{:S(2)}, u32[]{:S(2)}) collective-permute-start(f32[32,2048]{1,0:T(8,128)} %reduce-scatter.7.cloned.1.call-done), channel_id=1, source_target_pairs={{0,2},{2,0},{1,3},{3,1},{4,6},{6,4},{5,7},{7,5},{8,10},{10,8},{9,1... | collective-permute-start | bytes 786440 | tf_op jit(solution)/shard_map/ppermute | solution.py:58
  104.3 43.4 %collective-permute-start.2 = (f32[32,2048]{1,0:T(8,128)}, f32[32,2048]{1,0:T(8,128)S(1)}, u32[]{:S(2)}, u32[]{:S(2)}) collective-permute-start(f32[32,2048]{1,0:T(8,128)} %reduce-scatter.9.cloned.1.call-done), channel_id=1, source_target_pairs={{0,2},{2,0},{1,3},{3,1},{4,6},{6,4},{5,7},{7,5},{8,10},{10,8},{9,1... | collective-permute-start | bytes 786440 | tf_op jit(solution)/shard_map/ppermute | solution.py:58
  108.1 3.8 %copy-start = (f32[16,128,2,128]{3,2,1,0:T(2,128)S(1)}, f32[16,128,2,128]{3,2,1,0:T(2,128)}, u32[]{:S(2)}) copy-start(f32[16,128,2,128]{3,2,1,0:T(2,128)} %get-tuple-element.17) | copy-start | bytes 6291460
  108.1 3.8 %copy-start.1 = (f32[32,2048]{0,1:T(8,128)S(1)}, f32[32,2048]{0,1:T(8,128)}, u32[]{:S(2)}) copy-start(f32[32,2048]{0,1:T(8,128)} %copy.20) | copy-start | bytes 786436
  111.9 2.3 %copy-start.2 = (f32[32,2048]{0,1:T(8,128)S(1)}, f32[32,2048]{0,1:T(8,128)}, u32[]{:S(2)}) copy-start(f32[32,2048]{0,1:T(8,128)} %copy.23) | copy-start | bytes 786436
  132.3 22.5 %collective-permute-start.3 = (f32[32,2048]{1,0:T(8,128)}, f32[32,2048]{1,0:T(8,128)}, u32[]{:S(2)}, u32[]{:S(2)}) collective-permute-start(f32[32,2048]{1,0:T(8,128)} %reduce-scatter.11.cloned.1.call-done), channel_id=1, source_target_pairs={{0,2},{2,0},{1,3},{3,1},{4,6},{6,4},{5,7},{7,5},{8,10},{10,8},{9,1... | collective-permute-start | bytes 786440 | tf_op jit(solution)/shard_map/ppermute | solution.py:58
  140.1 1.3 copy-start.11
  140.1 1.3 copy-start.24
  144.5 1.3 copy-start.10
  148.0 1.6 copy-start.9
  148.0 2.6 %copy-start.19 = (f32[1,32,16,128]{3,2,0,1:T(8,128)S(1)}, f32[1,32,16,128]{3,2,0,1:T(8,128)}, u32[]{:S(2)}) copy-start(f32[1,32,16,128]{3,2,0,1:T(8,128)} %get-tuple-element.28) | copy-start | bytes 786436
  148.0 2.7 %copy-start.18 = (f32[1,32,16,128]{3,2,0,1:T(8,128)S(1)}, f32[1,32,16,128]{3,2,0,1:T(8,128)}, u32[]{:S(2)}) copy-start(f32[1,32,16,128]{3,2,0,1:T(8,128)} %get-tuple-element.27) | copy-start | bytes 786436
  149.6 1.9 copy-start.21
  149.6 2.7 %copy-start.20 = (f32[1,32,16,128]{3,2,0,1:T(8,128)S(1)}, f32[1,32,16,128]{3,2,0,1:T(8,128)}, u32[]{:S(2)}) copy-start(f32[1,32,16,128]{3,2,0,1:T(8,128)} %get-tuple-element.25) | copy-start | bytes 786436
  156.0 1.3 copy-start.8
  157.4 1.3 copy-start.6
  157.4 1.5 copy-start.7
  157.4 1.6 copy-start.13
  157.4 1.6 copy-start.15
  157.4 1.7 copy-start.17
  158.4 1.4 copy-start.4
  158.5 1.7 copy-start.5
  158.5 1.7 copy-start.14
  158.5 1.8 copy-start.16
Sparse Core Ops, SparseCore 0:
  18.0 29.9 reduce-scatter.4
  50.4 25.7 reduce-scatter.6
  78.5 25.7 reduce-scatter.8
  106.4 25.7 reduce-scatter.10

commit v2 on v1

v2 whole, which is shorter than its diff:
```python
import functools
import math

import jax
import jax.numpy as jnp
import numpy as np
from jax import lax
from jax.experimental import pallas as pl
from jax.experimental.pallas import tpu as pltpu
from jax.sharding import PartitionSpec as P

CHUNKS = 4
MESH = pl.DeviceIdType.MESH


def hint_kernel(cols, rows, a_ref, d_hbm, out_ref, d_buf, part, from_left, from_right,
                d_sem, send_sem, recv_sem, row_send, row_recv):
    me = lax.axis_index("col")
    row = lax.axis_index("row")
    own, width = part.shape[2:]
    has_left, has_right = me > 0, me < cols - 1
    loads = [
        pltpu.make_async_copy(d_hbm.at[pl.ds(k * width, width)], d_buf.at[k], d_sem.at[k])
        for k in range(CHUNKS)
    ]
    for load in loads:
        load.start()
    barrier = pltpu.get_barrier_semaphore()
    for there, side in ((has_left, -1), (has_right, 1)):
        @pl.when(there)
        def _():
            pl.semaphore_signal(barrier, inc=1, device_id={"col": me + side}, device_id_type=MESH)
    for step in range(1, rows):
        pl.semaphore_signal(
            barrier, inc=1, device_id={"row": lax.rem(row + step, rows)}, device_id_type=MESH
        )
    inner = has_left & has_right

    @pl.when(inner)
    def _():
        pl.semaphore_wait(barrier, rows + 1)

    @pl.when(jnp.logical_not(inner))
    def _():
        pl.semaphore_wait(barrier, rows - 1 + min(cols - 1, 1))

    def hop(k, d, side):
        landing = from_left if side > 0 else from_right
        lane = 0 if side > 0 else 1
        return pltpu.make_async_remote_copy(
            src_ref=part.at[k, d],
            dst_ref=landing.at[k, d],
            send_sem=send_sem.at[k, d],
            recv_sem=recv_sem.at[lane, k, d],
            device_id={"col": me + side},
            device_id_type=MESH,
        )

    def across(k, step):
        here = out_ref.at[row, :, pl.ds(k * width, width)]
        return pltpu.make_async_remote_copy(
            src_ref=here,
            dst_ref=here,
            send_sem=row_send.at[k, step - 1],
            recv_sem=row_recv.at[k, step - 1],
            device_id={"row": lax.rem(row + step, rows)},
            device_id_type=MESH,
        )

    for k in range(CHUNKS):
        loads[k].wait()
        part[k] = lax.dot_general(
            a_ref[...], d_buf[k], (((1,), (1,)), ((), ())), preferred_element_type=jnp.float32
        ).reshape(cols, own, width)

        @pl.when(me == 0)
        def _():
            for d in range(cols - 1, 0, -1):
                hop(k, d, 1).start()

        @pl.when(me == cols - 1)
        def _():
            for d in range(cols - 1):
                hop(k, d, -1).start()

    for k in range(CHUNKS):
        for i in range(cols - 1):
            right, left = cols - 1 - i, i

            @pl.when(has_left & (me < right))
            def _():
                hop(k, right, 1).wait_recv()
                part[k, right] += from_left[k, right]
                hop(k, right, 1).start()

            @pl.when(has_right & (me > left))
            def _():
                hop(k, left, -1).wait_recv()
                part[k, left] += from_right[k, left]
                hop(k, left, -1).start()

        @pl.when(has_left)
        def _():
            hop(k, me, 1).wait_recv()
            part[k, me] += from_left[k, me]

        @pl.when(has_right)
        def _():
            hop(k, me, -1).wait_recv()
            part[k, me] += from_right[k, me]

        out_ref[row, :, k * width : (k + 1) * width] = part[k, me]
        for step in range(1, rows):
            across(k, step).start()

    for k in range(CHUNKS):
        for d in range(cols):
            @pl.when(me != d)
            def _():
                hop(k, d, 1).wait_send()
        for step in range(1, rows):
            across(k, step).wait()


def gather_hint(panel, database, cols, rows):
    row_dev, depth = database.shape
    own, width = panel.shape[0] // cols, row_dev // CHUNKS
    blocks = pltpu.VMEM((CHUNKS, cols, own, width), jnp.float32)
    return pl.pallas_call(
        functools.partial(hint_kernel, cols, rows),
        out_shape=jax.ShapeDtypeStruct((rows, own, row_dev), jnp.float32),
        in_specs=[pl.BlockSpec(memory_space=pltpu.VMEM), pl.BlockSpec(memory_space=pl.ANY)],
        out_specs=pl.BlockSpec(memory_space=pltpu.VMEM),
        scratch_shapes=[
            pltpu.VMEM((CHUNKS, width, depth), database.dtype),
            blocks,
            blocks,
            blocks,
            pltpu.SemaphoreType.DMA((CHUNKS,)),
            pltpu.SemaphoreType.DMA((CHUNKS, cols)),
            pltpu.SemaphoreType.DMA((2, CHUNKS, cols)),
            pltpu.SemaphoreType.DMA((CHUNKS, max(rows - 1, 1))),
            pltpu.SemaphoreType.DMA((CHUNKS, max(rows - 1, 1))),
        ],
        compiler_params=pltpu.CompilerParams(
            collective_id=0, has_side_effects=True, vmem_limit_bytes=48 << 20
        ),
    )(panel, database)


def sum_kernel(cols, limbs, x_ref, out_ref, landed, send_sem, recv_sem):
    col, limb = lax.axis_index("col"), lax.axis_index("limb")
    count = cols * limbs
    me = col * limbs + limb
    peers = [lax.rem(me + step, count) for step in range(1, count)]
    barrier = pltpu.get_barrier_semaphore()
    copies = []
    for step, peer in enumerate(peers):
        where = {"col": peer // limbs, "limb": lax.rem(peer, limbs)}
        pl.semaphore_signal(barrier, inc=1, device_id=where, device_id_type=MESH)
        copies.append(
            pltpu.make_async_remote_copy(
                src_ref=x_ref,
                dst_ref=landed.at[step],
                send_sem=send_sem.at[step],
                recv_sem=recv_sem.at[step],
                device_id=where,
                device_id_type=MESH,
            )
        )
    pl.semaphore_wait(barrier, count - 1)
    for copy in copies:
        copy.start()
    total = x_ref[...]
    for step, copy in enumerate(copies):
        copy.wait()
        total = total + landed[step]
    out_ref[...] = total


def sum_all(x, cols, limbs):
    peers = cols * limbs - 1
    return pl.pallas_call(
        functools.partial(sum_kernel, cols, limbs),
        out_shape=jax.ShapeDtypeStruct(x.shape, x.dtype),
        in_specs=[pl.BlockSpec(memory_space=pltpu.VMEM)],
        out_specs=pl.BlockSpec(memory_space=pltpu.VMEM),
        scratch_shapes=[
            pltpu.VMEM((peers,) + x.shape, x.dtype),
            pltpu.SemaphoreType.DMA((peers,)),
            pltpu.SemaphoreType.DMA((peers,)),
        ],
        compiler_params=pltpu.CompilerParams(collective_id=1, has_side_effects=True),
    )(x)


def tables(row_count, row_dev, fast):
    slow = row_dev // fast
    degree = row_count * row_dev
    m = np.arange(row_dev)
    t = np.arange(fast)
    angle = -2.0 * np.pi * (m[:, None] * t[None, :] % row_dev) / row_dev
    first = np.exp(1j * angle).reshape(fast, slow, fast).transpose(1, 0, 2)
    a = np.arange(row_count)
    n = np.arange(degree)
    turn = -np.pi * (n[None, :] * (2 * a[:, None] + 1) % (2 * degree)) / degree
    turn = np.exp(1j * turn).reshape(row_count, row_count, fast, slow).transpose(0, 3, 1, 2)
    v = np.arange(slow)
    last = np.exp(-2j * np.pi * (v[:, None] * v[None, :] % slow) / slow)
    last = np.stack([np.stack([last.real, last.imag], 0), np.stack([-last.imag, last.real], 0)], 0)
    return first, turn, last.astype(np.float32)


def body(database, lwe_matrix, secret_ct):
    row_count = lax.axis_size("row")
    row_rank = lax.axis_index("row")
    col_count = lax.axis_size("col")
    row_dev = database.shape[0]
    half = lwe_matrix.shape[2]
    own = half // col_count
    fast = 128
    slow = row_dev // fast
    first, turn, last = tables(row_count, row_dev, fast)
    f_re = jnp.asarray(first.real, jnp.float32)[:, None]
    f_im = jnp.asarray(first.imag, jnp.float32)[:, None]
    g_re = lax.dynamic_index_in_dim(jnp.asarray(turn.real, jnp.float32), row_rank, 0, False)[..., None]
    g_im = lax.dynamic_index_in_dim(jnp.asarray(turn.imag, jnp.float32), row_rank, 0, False)[..., None]
    stage = jnp.stack([f_re * g_re - f_im * g_im, f_re * g_im + f_im * g_re], axis=3)
    stage = stage.reshape(slow, row_count, fast, 2, fast)
    blocks = gather_hint(lwe_matrix[:, 0, :].T, database, col_count, row_count)
    total = 0.0
    for source in range(row_count):
        total = total + jnp.einsum(
            "juv,vuct->vjct",
            blocks[source].reshape(own, fast, slow),
            stage[:, source],
            precision=lax.Precision.HIGH,
            preferred_element_type=jnp.float32,
        )
    spec = jnp.einsum("vjct,cdvs->djst", total, last, precision=lax.Precision.HIGH)
    spec = spec.reshape(2, own, row_dev)
    scale = 1.0 / (math.sqrt(row_dev * row_count) * math.sqrt(2 * half))
    cipher = secret_ct[:, :, 0]
    prod_real = jnp.sum(spec[0] * cipher[:, 0] - spec[1] * cipher[:, 1], axis=1)
    prod_imag = jnp.sum(spec[0] * cipher[:, 1] + spec[1] * cipher[:, 0], axis=1)
    product = jnp.concatenate([prod_real, prod_imag], axis=0) * scale
    product = sum_all(
        product.reshape(8, -1), col_count, lax.axis_size("limb")
    ).reshape(2, 2, row_dev)
    return jnp.swapaxes(product, 0, 1)


def solution(mesh):
    placed = (P(("grp", "row"), "col"), P("col", "limb", None), P(None, None, "limb", "col", "row"))
    return jax.shard_map(
        body, mesh=mesh, in_specs=placed, out_specs=P("grp", None, "row"), check_vma=False
    )
```

time: 195 us -> 138 us (0.71)
  Pallas kernels: 0 us -> 99.4 us
  waiting for transfers between devices: 52.5 us -> 0 us
  matrix products: 50.9 us -> 9.28 us
  blocking collectives: 25.9 us -> 0 us
  local copies, waits for them, and re-layouts: 25.3 us -> 11.1 us
  between operations: 13.6 us -> 0.13 us
  starting transfers between devices: 7.37 us -> 0 us
    pallas_call x0 -> x2, Pallas kernels: none -> 99.4 us  [the longest x1 90.2 us: gather_hint(): pl.pallas_call(functools.partial(hint_kernel, cols, rows), out_shape=jax....]
    reduce_scatter x4 -> x0, waiting for transfers between devices: 52.4 us -> none  [body(): mine = lax.psum_scatter(partial, 'col', scatter_dimension=0, tiled=True)]
    dot_general x12 -> x2, matrix products: 47 us -> 5.78 us  [body(): jnp.einsum('juv,vuct->vjct', blocks[source].reshape(own, fast, slow), sta...]
    psum x1 -> x0, blocking collectives: 25.9 us -> none  [body(): lax.psum(jnp.stack([prod_real, prod_imag], axis=1) * scale, ('col', 'limb'))]
    sub x0 -> x1, other arithmetic: none -> 11 us  [body(): f_re * g_re - f_im * g_im]
    add x3 -> x0, other arithmetic: 10.8 us -> none  [the longest x1 10.7 us: body(): f_re * g_im + f_im * g_re]
    reduce_scatter x4 -> x0, local copies, waits for them, and re-layouts: 7.35 us -> none  [body(): mine = lax.psum_scatter(partial, 'col', scatter_dimension=0, tiled=True)]
    ppermute x4 -> x0, starting transfers between devices: 7.24 us -> none  [body(): blocks.append(lax.ppermute(mine, 'row', perm))]
  transfers between devices with their start and end apart: 8 -> 0, of which waited for: 3 -> 0; matrix products, arithmetic and copies ran while one was open for 39% -> 0% of each run, Pallas kernels for 0% -> 0%
where the time goes in v2:
time: 138 us; the launch traced here: 137 us
  Pallas kernels  99.4 us (72%)
  other arithmetic  17 us (12%)
  local copies, waits for them, and re-layouts  11.1 us (8%)
  matrix products  9.28 us (7%)
    pallas_call x1, Pallas kernels, gather_hint(): pl.pallas_call(functools.partial(hint_kernel, cols, rows), out_shape=jax....  90.2 us
    sub x1, other arithmetic, body(): f_re * g_re - f_im * g_im  11 us
    pallas_call x1, Pallas kernels, sum_all(): pl.pallas_call(functools.partial(sum_kernel, cols, limbs), out_shape=jax....  9.23 us
    dot_general x2, matrix products, body(): jnp.einsum('juv,vuct->vjct', blocks[source].reshape(own, fast, slow), sta...  5.78 us
    squeeze x1, other arithmetic, body(): stage[:, source]  5.13 us
    unnamed x7, local copies, waits for them, and re-layouts  5.1 us
    dot_general x1, matrix products, body(): jnp.einsum('vjct,cdvs->djst', total, last, precision=lax.Precision.HIGH)  3.5 us
    slice x3, local copies, waits for them, and re-layouts, body(): blocks[source].reshape(own, fast, slow)  3.04 us

profile of v2, /device:TPU:0, one launch (start us, length us, event | category | flops | bytes accessed | tf_op | source)
XLA Modules:
  0.0 136.9 jit_solution(6138142170689179481)
XLA Ops:
  0.0 0.7 dynamic-slice_bitcast_fusion
  0.7 11.0 %multiply_subtract_fusion = (f32[16,2,128,1,128]{4,3,2,1,0:T(1,128)S(1)}, f32[16,2,128,1,128]{4,3,2,1,0:T(1,128)S(1)}) fusion(f32[16,2,128]{2,1,0:T(2,128)S(1)} %get-tuple-element.15, f32[16,128,128]{2,1,0:T(8,128)} %constant.27.clone, f32[16,2,128]{2,1,0:T(2,128)S(1)} %get-tuple-element.16, f32[16,128,128]{2,1,0:T(8,128)} %constant.26.clone), kind=kLoop, calls=%fused_computation.19 | loop fusion | flops 3145728 | bytes 6324224 | tf_op jit(solution)/shard_map/sub | solution.py:228
  11.8 5.1 %fusion.1 = (f32[16,128,2,128]{3,2,1,0:T(2,128)}, f32[16,128,2,128]{3,2,1,0:T(2,128)}) fusion(f32[16,2,128,1,128]{4,3,2,1,0:T(1,128)S(1)} %get-tuple-element.9, f32[16,2,128,1,128]{4,3,2,1,0:T(1,128)S(1)} %get-tuple-element.10), kind=kLoop, calls=%fused_computation.3 | loop fusion | flops 1048576 | bytes 8388608 | tf_op jit(solution)/shard_map/squeeze | solution.py:236
  16.9 2.9 %copy.12 = bf16[2048,1,512]{0,2,1:T(8,128)(2,1)S(1)} copy(bf16[2048,1,512]{2,0,1:T(8,128)(2,1)} %param.9) | data formatting | bytes 4194304 | tf_op args[1]
  19.8 90.2 %shard_map.82 = f32[2,128,2048]{2,1,0:T(8,128)S(1)} custom-call(bf16[512,2048]{1,0:T(8,128)(2,1)S(1)} %bitcast.61, bf16[2048,2048]{1,0:T(8,128)(2,1)} %d_hbm.1), custom_call_target="tpu_custom_call" | custom-call | tf_op jit(solution)/shard_map/pallas_call | solution.py:129
  110.1 1.2 fusion.16
  111.2 0.3 copy.14
  111.6 2.9 %fusion.5 = f32[16,128,2,128]{3,1,2,0:T(8,128)S(1)} fusion(f32[16,128,2,128]{3,2,1,0:T(2,128)} %get-tuple-element.8, f32[128,128,16,1]{0,2,1,3:T(8,128)S(1)} %bitcast.62), kind=kOutput, calls=%fused_computation.11 | convolution fusion | flops 402653184 | bytes 5242880 | tf_op jit(solution)/shard_map/juv,vuct->vjct/dot_general | solution.py:233
  114.4 1.5 %copy.13 = f32[1,128,2048]{1,2,0:T(8,128)S(1)} copy(f32[1,128,2048]{2,1,0:T(8,128)} %get-tuple-element.13) | data formatting | bytes 2097152 | tf_op jit(solution)/shard_map/slice | solution.py:235
  116.0 0.0 copy-start.1
  116.0 2.9 %fusion.8 = f32[16,128,2,128]{3,1,2,0:T(8,128)S(1)} fusion(f32[16,128,2,128]{3,2,1,0:T(2,128)} %get-tuple-element.7, f32[128,128,16,1]{0,2,1,3:T(8,128)S(1)} %bitcast.63), kind=kOutput, calls=%fused_computation.14 | convolution fusion | flops 402653184 | bytes 5242880 | tf_op jit(solution)/shard_map/juv,vuct->vjct/dot_general | solution.py:233
  118.9 0.0 copy-done.1
  118.9 3.5 %fusion.10 = f32[2,128,16,128]{3,2,0,1:T(8,128)S(1)} fusion(f32[2,2,16,16,1]{2,3,0,1,4:T(8,128)S(1)} %copy-done.1, f32[16,128,2,128]{3,1,2,0:T(8,128)S(1)} %fusion.5, f32[16,128,2,128]{3,1,2,0:T(8,128)S(1)} %fusion.8), kind=kOutput, calls=%fused_computation.20 | convolution fusion | flops 101187584 | bytes 6295552 | tf_op jit(solution)/shard_map/vjct,cdvs->djst/dot_general | solution.py:240
  122.4 0.2 fusion.15
  122.6 0.0 copy-start
  122.6 0.3 copy.51
  123.0 0.3 copy.52
  123.3 1.5 %copy-done = f32[2,2,1,128,2048]{4,3,2,1,0:T(8,128)S(1)} copy-done((f32[2,2,1,128,2048]{4,3,2,1,0:T(8,128)S(1)}, f32[2,2,1,128,2048]{4,3,2,1,0:T(8,128)}, u32[]{:S(2)}) %copy-start) | copy-done | bytes 4194328
  124.8 0.8 subtract_reduce_fusion
  125.6 0.6 mul.138.x_ref
  126.3 9.2 %shard_map.83 = f32[8,1024]{1,0:T(8,128)} custom-call(f32[8,1024]{1,0:T(8,128)} %mul.138.x_ref), custom_call_target="tpu_custom_call" | custom-call | tf_op jit(solution)/shard_map/pallas_call | solution.py:183
  135.5 0.8 reshape.36
  136.3 0.6 copy.53
  (1 shorter events, 0.0 us)
Async XLA Ops:
  116.0 2.9 %copy-start.1 = (f32[2,2,16,16,1]{2,3,0,1,4:T(8,128)S(1)}, f32[2,2,16,16,1]{2,3,0,1,4:T(8,128)}, u32[]{:S(2)}) copy-start(f32[2,2,16,16,1]{2,3,0,1,4:T(8,128)} %constant.33) | copy-start | bytes 12292
  122.6 2.2 %copy-start = (f32[2,2,1,128,2048]{4,3,2,1,0:T(8,128)S(1)}, f32[2,2,1,128,2048]{4,3,2,1,0:T(8,128)}, u32[]{:S(2)}) copy-start(f32[2,2,1,128,2048]{4,3,2,1,0:T(8,128)} %param.10) | copy-start | bytes 12582916

commit v3 on v2

--- a/solution.py
+++ b/solution.py
@@ -201,14 +201,18 @@
     t = np.arange(fast)
     angle = -2.0 * np.pi * (m[:, None] * t[None, :] % row_dev) / row_dev
     first = np.exp(1j * angle).reshape(fast, slow, fast).transpose(1, 0, 2)
+    first = np.stack([first.real, first.imag], 2).astype(np.float32)
     a = np.arange(row_count)
     n = np.arange(degree)
     turn = -np.pi * (n[None, :] * (2 * a[:, None] + 1) % (2 * degree)) / degree
-    turn = np.exp(1j * turn).reshape(row_count, row_count, fast, slow).transpose(0, 3, 1, 2)
+    turn = np.exp(1j * turn).reshape(row_count, row_count, row_dev)
+    turn = np.stack([turn.real, turn.imag], 1).astype(np.float32)
     v = np.arange(slow)
     last = np.exp(-2j * np.pi * (v[:, None] * v[None, :] % slow) / slow)
-    last = np.stack([np.stack([last.real, last.imag], 0), np.stack([-last.imag, last.real], 0)], 0)
-    return first, turn, last.astype(np.float32)
+    last = np.stack([last, 1j * last], 0)
+    last = np.stack([last, 1j * last], 0)
+    last = np.stack([last.real, last.imag], 2).astype(np.float32)
+    return first, turn, last
 
 
 def body(database, lwe_matrix, secret_ct):
@@ -221,23 +225,17 @@
     fast = 128
     slow = row_dev // fast
     first, turn, last = tables(row_count, row_dev, fast)
-    f_re = jnp.asarray(first.real, jnp.float32)[:, None]
-    f_im = jnp.asarray(first.imag, jnp.float32)[:, None]
-    g_re = lax.dynamic_index_in_dim(jnp.asarray(turn.real, jnp.float32), row_rank, 0, False)[..., None]
-    g_im = lax.dynamic_index_in_dim(jnp.asarray(turn.imag, jnp.float32), row_rank, 0, False)[..., None]
-    stage = jnp.stack([f_re * g_re - f_im * g_im, f_re * g_im + f_im * g_re], axis=3)
-    stage = stage.reshape(slow, row_count, fast, 2, fast)
     blocks = gather_hint(lwe_matrix[:, 0, :].T, database, col_count, row_count)
-    total = 0.0
-    for source in range(row_count):
-        total = total + jnp.einsum(
-            "juv,vuct->vjct",
-            blocks[source].reshape(own, fast, slow),
-            stage[:, source],
-            precision=lax.Precision.HIGH,
-            preferred_element_type=jnp.float32,
-        )
-    spec = jnp.einsum("vjct,cdvs->djst", total, last, precision=lax.Precision.HIGH)
+    turn = lax.dynamic_index_in_dim(jnp.asarray(turn), row_rank, 0, False)
+    turned = jnp.sum(blocks[None] * turn[:, :, None, :], axis=1)
+    total = jnp.einsum(
+        "zjuv,vuct->vzjct",
+        turned.reshape(2, own, fast, slow),
+        first,
+        precision=lax.Precision.HIGH,
+        preferred_element_type=jnp.float32,
+    )
+    spec = jnp.einsum("vzjct,zcdvs->djst", total, last, precision=lax.Precision.HIGH)
     spec = spec.reshape(2, own, row_dev)
     scale = 1.0 / (math.sqrt(row_dev * row_count) * math.sqrt(2 * half))
     cipher = secret_ct[:, :, 0]

time: 138 us -> 119 us (0.86)
  other arithmetic: 17 us -> 1.23 us
    sub x1 -> x0, other arithmetic: 11 us -> none  [body(): f_re * g_re - f_im * g_im]
    squeeze x1 -> x0, other arithmetic: 5.13 us -> none  [body(): stage[:, source]]
    slice x3 -> x0, local copies, waits for them, and re-layouts: 3.04 us -> none  [body(): blocks[source].reshape(own, fast, slow)]
    reduce_sum x0 -> x1, local copies, waits for them, and re-layouts: none -> 1.87 us  [body(): turned = jnp.sum(blocks[None] * turn[:, :, None, :], axis=1)]
    dot_general x3 -> x2, matrix products: 9.28 us -> 8 us  [the longest x1 4.57 us: body(): jnp.einsum('zjuv,vuct->vzjct', turned.reshape(2, own, fast, slow), first,...]
    unnamed x7 -> x5, local copies, waits for them, and re-layouts: 5.1 us -> 4.21 us
where the time goes in v3:
time: 119 us
  Pallas kernels  99.4 us (84%)
  local copies, waits for them, and re-layouts  9.95 us (8%)
  matrix products  8 us (7%)
  other arithmetic  1.23 us (1%)
    pallas_call x1, Pallas kernels, gather_hint(): pl.pallas_call(functools.partial(hint_kernel, cols, rows), out_shape=jax....  90.2 us
    pallas_call x1, Pallas kernels, sum_all(): pl.pallas_call(functools.partial(sum_kernel, cols, limbs), out_shape=jax....  9.22 us
    dot_general x1, matrix products, body(): jnp.einsum('zjuv,vuct->vzjct', turned.reshape(2, own, fast, slow), first,...  4.57 us
    unnamed x5, local copies, waits for them, and re-layouts  4.21 us
    dot_general x1, matrix products, body(): jnp.einsum('vzjct,zcdvs->djst', total, last, precision=lax.Precision.HIGH)  3.43 us

profile of v3, /device:TPU:0, one launch (start us, length us, event | category | flops | bytes accessed | tf_op | source)
XLA Modules:
  0.0 118.7 jit_solution(2485836052432258754)
XLA Ops:
  0.0 0.8 dynamic-slice_bitcast_fusion
  0.8 2.9 %copy.13 = bf16[2048,1,512]{0,2,1:T(8,128)(2,1)S(1)} copy(bf16[2048,1,512]{2,0,1:T(8,128)(2,1)} %param.7) | data formatting | bytes 4194304 | tf_op args[1]
  3.7 90.2 %shard_map.64 = f32[2,128,2048]{2,1,0:T(8,128)S(1)} custom-call(bf16[512,2048]{1,0:T(8,128)(2,1)S(1)} %bitcast.50, bf16[2048,2048]{1,0:T(8,128)(2,1)} %d_hbm.1), custom_call_target="tpu_custom_call" | custom-call | tf_op jit(solution)/shard_map/pallas_call | solution.py:129
  93.9 0.4 multiply_reduce_fusion
  94.3 1.9 %copy.14 = f32[2,128,2048]{1,2,0:T(8,128)} copy(f32[2,128,2048]{2,1,0:T(8,128)S(1)} %multiply_reduce_fusion) | data formatting | bytes 4194304 | tf_op jit(solution)/shard_map/reduce_sum | solution.py:230
  96.2 0.0 copy-start.1
  96.2 4.6 %convolution_bitcast_fusion = f32[16,2,128,2,128,1]{4,2,3,1,0,5:T(8,128)S(1)} fusion(f32[16,128,2,128,1]{3,1,2,4,0:T(8,128)} %constant.25, f32[2,128,128,16,1]{1,3,2,0,4:T(8,128)} %bitcast.51), kind=kOutput, calls=%fused_computation.3 | convolution fusion | flops 805306368 | bytes 8388608 | tf_op jit(solution)/shard_map/zjuv,vuct->vzjct/dot_general | solution.py:231
  100.8 0.0 copy-done.1
  100.8 3.4 %fusion.3 = f32[2,128,16,128]{3,2,0,1:T(8,128)S(1)} fusion(f32[2,2,2,16,16,1]{3,4,0,1,2,5:T(8,128)S(1)} %copy-done.1, f32[16,2,128,2,128,1]{4,2,3,1,0,5:T(8,128)S(1)} %convolution_bitcast_fusion), kind=kOutput, calls=%fused_computation.9 | convolution fusion | flops 201326592 | bytes 6299648 | tf_op jit(solution)/shard_map/vzjct,zcdvs->djst/dot_general | solution.py:238
  104.2 0.2 fusion.6
  104.4 0.0 copy-start
  104.4 0.9 copy_bitcast_fusion
  105.3 1.3 %copy-done = f32[2,2,1,128,2048]{4,3,2,1,0:T(8,128)S(1)} copy-done((f32[2,2,1,128,2048]{4,3,2,1,0:T(8,128)S(1)}, f32[2,2,1,128,2048]{4,3,2,1,0:T(8,128)}, u32[]{:S(2)}) %copy-start) | copy-done | bytes 4194328
  106.6 0.8 subtract_reduce_fusion
  107.4 0.6 mul.71.x_ref
  108.0 9.2 %shard_map.65 = f32[8,1024]{1,0:T(8,128)} custom-call(f32[8,1024]{1,0:T(8,128)} %mul.71.x_ref), custom_call_target="tpu_custom_call" | custom-call | tf_op jit(solution)/shard_map/pallas_call | solution.py:183
  117.3 0.8 reshape.19
  118.1 0.6 copy.39
  (1 shorter events, 0.0 us)
Async XLA Ops:
  96.2 4.6 %copy-start.1 = (f32[2,2,2,16,16,1]{3,4,0,1,2,5:T(8,128)S(1)}, f32[2,2,2,16,16,1]{3,4,0,1,2,5:T(8,128)}, u32[]{:S(2)}) copy-start(f32[2,2,2,16,16,1]{3,4,0,1,2,5:T(8,128)} %constant.26) | copy-start | bytes 24580
  104.4 2.2 %copy-start = (f32[2,2,1,128,2048]{4,3,2,1,0:T(8,128)S(1)}, f32[2,2,1,128,2048]{4,3,2,1,0:T(8,128)}, u32[]{:S(2)}) copy-start(f32[2,2,1,128,2048]{4,3,2,1,0:T(8,128)} %param.8) | copy-start | bytes 12582916
